TPU v7x, 256 devices: a whole 4x4x8 slice. The times are simulated.
256 devices in a mesh: ia: 4 (over y), ja: 4 (over x), ka: 16 (over z, core).
Axes of the slice: x: 4, y: 4, z: 8, core: 2. Of those that a mesh axis runs over, the one named last changes fastest.
Arguments:
- blocks: bfloat16 [4, 4, 16, 2, 128, 128, 128], P('ia', 'ja', 'ka'), may hold values from -6 to 6
- first_mode_rows: int32 [4, 4, 16, 2], P('ia', 'ja', 'ka'), may hold values from 0 to 15
- second_mode_rows: int32 [4, 4, 16, 2], P('ia', 'ja', 'ka'), may hold values from 0 to 15
- third_mode_rows: int32 [4, 4, 16, 2], P('ia', 'ja', 'ka'), may hold values from 0 to 3
- filled: int32 [4, 4, 16], P('ia', 'ja', 'ka'), may hold values from 1 to 2, as said below
- owner_one: int32 [64], replicated, may hold values from 0 to 63, each once
- owner_two: int32 [64], replicated, may hold values from 0 to 63, each once
- factor_b: float32 [4, 2048, 256], P('ja', ('ia', 'ka'))
- factor_c: float32 [16, 512, 256], P('ka')
Outputs:
- a_new: float32 [4, 2048, 256], P('ia', ('ja', 'ka'))
- b_new: float32 [4, 2048, 256], P('ja', ('ia', 'ka'))
Inputs may be any that keep to these rules, and one draw needn't show every extreme that they name: Number of nonempty slots of a grid cell; at least one cell has all 2 slots filled. Slots at or beyond this count hold data that is not part of the tensor.
All inputs are finite; a program needn't handle non-finite values.
Results may differ from a plain program's by a relative error of at most 0.0039.
The roundings to bfloat16 on the way count: a program that leaves them out, or rounds other values in their place, can miss the bound.
Values may be sent and summed in bfloat16 or wider, within the bound.
A program may use at most 128 MiB of HBM per device.

v0:
```python
import jax
import jax.numpy as jnp
from jax import lax
from jax.sharding import PartitionSpec as P

EPS = 1e-06


def solve_rows(gram, rows):
    lower = jnp.linalg.cholesky(gram)
    return jax.scipy.linalg.cho_solve((lower, True), rows.T).T


def add_rows(accum, start, contrib):
    current = lax.dynamic_slice_in_dim(accum, start, contrib.shape[0], 0)
    return lax.dynamic_update_slice_in_dim(accum, current + contrib, start, 0)


def batched_sum(inner, weights):
    summed = lax.dot_general(
        inner,
        weights.astype(jnp.float32),
        (((1,), (0,)), ((2,), (1,))),
        precision=lax.Precision.HIGHEST,
        preferred_element_type=jnp.float32,
    )
    return summed.T


def to_logical(stored, owner, piece_rows):
    return stored.reshape(-1, piece_rows, stored.shape[1])[owner].reshape(stored.shape)


def to_stored(logical, owner, piece_rows):
    positions = jnp.arange(owner.shape[0], dtype=jnp.int32)
    inverse = jnp.sum(
        jnp.where(owner[None, :] == positions[:, None], positions[None, :], 0), axis=1
    )
    return logical.reshape(-1, piece_rows, logical.shape[1])[inverse].reshape(logical.shape)


def keep_same(value):
    return value


def partial_value(function, slot):

    def applied(value):
        return function(value, slot)

    return applied


def body(
    blocks,
    first_mode_rows,
    second_mode_rows,
    third_mode_rows,
    filled,
    owner_one,
    owner_two,
    factor_b,
    factor_c,
):
    highest = lax.Precision.HIGHEST
    piece_rows = factor_b.shape[1]
    rank_width = factor_b.shape[2]
    block_edge = blocks.shape[-1]
    slot_count = blocks.shape[3]
    total_one = piece_rows * lax.axis_size("ia") * lax.axis_size("ja") * lax.axis_size("ka")
    slab_rows_one = piece_rows * lax.axis_size("ja") * lax.axis_size("ka")
    slab_rows_two = piece_rows * lax.axis_size("ia") * lax.axis_size("ka")
    own_b = factor_b[0]
    own_c = lax.dynamic_slice_in_dim(
        factor_c[0], lax.axis_index(("ia", "ja")) * piece_rows, piece_rows, 0
    )
    local_b = jnp.dot(own_b.T, own_b, precision=highest, preferred_element_type=jnp.float32)
    local_c = jnp.dot(own_c.T, own_c, precision=highest, preferred_element_type=jnp.float32)
    gram_b, gram_c = lax.psum((local_b, local_c), ("ia", "ja", "ka"))
    stored_b = lax.all_gather(factor_b.astype(jnp.bfloat16), ("ia", "ka"), axis=1, tiled=True)[0]
    half_b = to_logical(stored_b, owner_two, piece_rows)
    half_c = factor_c[0].astype(jnp.bfloat16)
    live_count = filled[0, 0, 0]

    def update_one(partial_sum, slot):
        block = blocks[0, 0, 0, slot]
        b_rows = lax.dynamic_slice_in_dim(
            half_b, second_mode_rows[0, 0, 0, slot] * block_edge, block_edge, 0
        )
        c_rows = lax.dynamic_slice_in_dim(
            half_c, third_mode_rows[0, 0, 0, slot] * block_edge, block_edge, 0
        )
        inner = jnp.dot(
            block.reshape(block_edge * block_edge, block_edge),
            c_rows,
            preferred_element_type=jnp.float32,
        )
        inner = inner.reshape(block_edge, block_edge, rank_width)
        contrib = batched_sum(inner, b_rows)
        return add_rows(partial_sum, first_mode_rows[0, 0, 0, slot] * block_edge, contrib)

    partial_one = jnp.zeros((slab_rows_one, rank_width), jnp.float32)
    for slot in range(slot_count):
        partial_one = lax.cond(
            slot < live_count, partial_value(update_one, slot), keep_same, partial_one
        )
    stored_one = to_stored(partial_one, owner_one, piece_rows)
    system_one = gram_b * gram_c
    summed_own = lax.psum_scatter(stored_one, ("ja", "ka"), scatter_dimension=0, tiled=True)
    a_hat = solve_rows(system_one, summed_own)
    squares_a = lax.psum(jnp.sum(a_hat * a_hat, axis=0), ("ia", "ja", "ka"))
    scale_a = jnp.sqrt(squares_a / total_one + EPS)
    a_own = a_hat / scale_a
    local_a = jnp.dot(a_own.T, a_own, precision=highest, preferred_element_type=jnp.float32)
    gram_a = lax.psum(local_a, ("ia", "ja", "ka"))
    stored_a = lax.all_gather(a_own.astype(jnp.bfloat16)[None], ("ja", "ka"), axis=1, tiled=True)[0]
    half_a = to_logical(stored_a, owner_one, piece_rows)

    def update_two(partial_sum, slot):
        block = blocks[0, 0, 0, slot]
        a_rows = lax.dynamic_slice_in_dim(
            half_a, first_mode_rows[0, 0, 0, slot] * block_edge, block_edge, 0
        )
        c_rows = lax.dynamic_slice_in_dim(
            half_c, third_mode_rows[0, 0, 0, slot] * block_edge, block_edge, 0
        )
        inner = lax.dot_general(
            block.reshape(block_edge, block_edge * block_edge),
            a_rows,
            (((0,), (0,)), ((), ())),
            preferred_element_type=jnp.float32,
        )
        inner = inner.reshape(block_edge, block_edge, rank_width)
        contrib = batched_sum(inner, c_rows)
        return add_rows(partial_sum, second_mode_rows[0, 0, 0, slot] * block_edge, contrib)

    partial_two = jnp.zeros((slab_rows_two, rank_width), jnp.float32)
    for slot in range(slot_count):
        partial_two = lax.cond(
            slot < live_count, partial_value(update_two, slot), keep_same, partial_two
        )
    stored_two = to_stored(partial_two, owner_two, piece_rows)
    summed_two = lax.psum_scatter(stored_two, ("ia", "ka"), scatter_dimension=0, tiled=True)
    b_hat = solve_rows(gram_a * gram_c, summed_two)
    squares_b = lax.psum(jnp.sum(b_hat * b_hat, axis=0), ("ia", "ja", "ka"))
    b_own = b_hat / jnp.sqrt(squares_b / total_one + EPS)
    return (a_own[None], b_own[None])


def solution(mesh):
    return jax.shard_map(
        body,
        mesh=mesh,
        in_specs=(
            P("ia", "ja", "ka", None, None, None, None),
            P("ia", "ja", "ka", None),
            P("ia", "ja", "ka", None),
            P("ia", "ja", "ka", None),
            P("ia", "ja", "ka"),
            P(),
            P(),
            P("ja", ("ia", "ka"), None),
            P("ka", None, None),
        ),
        out_specs=(P("ia", ("ja", "ka"), None), P("ja", ("ia", "ka"), None)),
        check_vma=False,
    )
```

profile of v0, /device:TPU:1, one launch (start us, length us, event | category | flops | bytes accessed | tf_op | source)
XLA Modules:
  0.0 827.5 jit_solution(4852424667202017735)
XLA Ops:
  8.0 1.4 convert_element_type.36
  9.5 2.0 fusion.34
  11.5 2.0 fusion.36
  13.5 0.7 compare_select_fusion.3
  14.2 0.8 select_reduce_fusion.4
  14.9 0.8 select_reduce_fusion.5
  16.4 1.1 convert_bitcast_fusion
  17.5 75.5 %all-gather.4.cloned.1.call-done = bf16[1,2048,256]{2,1,0:T(8,128)(2,1)} async-done(((bf16[1,32,256]{2,1,0:T(8,128)(2,1)}), bf16[1,2048,256]{2,1,0:T(8,128)(2,1)}) %all-gather.4.cloned.1.call-update) | async-done | bytes 1048592 | tf_op jit(solution)/shard_map/all_gather | solution.py:80
  93.0 1.8 gather_fusion
  94.8 23.3 %conditional.4 = (f32[2048,256]{1,0:T(8,128)}) conditional(s32[]{:T(128)} %bitcast.41, () %tuple.54, (s32[1,1,1,2]{3,2,1,0:T(1,128)}, bf16[512,256]{1,0:T(8,128)(2,1)S(1)}, bf16[1,1,1,2,128,128,128]{6,5,4,3,2,1,0:T(8,128)(2,1)}, s32[1,1,1,2]{3,2,1,0:T(1,128)}, bf16[2048,256]{1,0:T(8,128)(2,1)S(1)}, /*index=5*/s32[1,1,1,2]{3,2,1,0:T(1,128)}) %tuple.134), branch_computations={%region_6.0_spmd, %region_7.0_spmd} | conditional | flops 1082130432 | bytes 83099928 | solution.py:104
  95.5 2.8 slice.76
  98.3 2.4 convolution_bitcast_fusion
  100.7 6.7 copy.52
  107.6 8.2 multiply_reduce_fusion
  116.0 1.5 broadcast.140
  117.4 0.7 bitcast_dynamic-update-slice_fusion.2
  118.1 3.6 gather_fusion.1
  121.8 0.3 all-gather.6.cloned.1.call-start
  122.1 149.6 %all-reduce.7.cloned.1.call-done = (f32[256,256]{0,1:T(8,128)}, f32[256,256]{0,1:T(8,128)}) async-done(((f32[256,256]{0,1:T(8,128)}, f32[256,256]{0,1:T(8,128)}), (f32[256,256]{0,1:T(8,128)}, f32[256,256]{0,1:T(8,128)})) %all-reduce.7.cloned.1.call-update) | async-done | bytes 524304 | tf_op jit(solution)/shard_map/psum | solution.py:79
  271.6 1.1 mul.94
  272.9 11.7 %cholesky.130 = f32[128,128]{1,0:T(8,128)S(1)} custom-call(f32[128,128]{1,0:T(8,128)S(1)} %cholesky.194), custom_call_target="Cholesky" | custom-call | tf_op jit(solution)/shard_map/jit(cholesky)/cholesky | solution.py:10
  284.7 9.8 %custom-call.15 = f32[1,128,128]{1,2,0:T(8,128)S(1)} custom-call(f32[1,128,128]{2,1,0:T(8,128)S(1)} %get-tuple-element.155), custom_call_target="InvertDiagBlocksLowerTriangular" | custom-call | tf_op jit(solution)/shard_map/jit(cholesky)/cholesky | solution.py:10
  295.0 11.7 %cholesky.147 = f32[128,128]{1,0:T(8,128)S(1)} custom-call(f32[128,128]{1,0:T(8,128)S(1)} %convolution_subtract_fusion.1), custom_call_target="Cholesky" | custom-call | tf_op jit(solution)/shard_map/jit(cholesky)/cholesky | solution.py:10
  306.8 0.7 compare_reduce_fusion.2
  308.8 14.6 %while.4 = (s32[]{:T(128)}, f32[256,256]{1,0:T(8,128)S(1)}, s32[2,2]{1,0:T(2,128)S(1)}, f32[2,128,128]{2,1,0:T(8,128)S(1)}, s32[]{:T(128)}) while((s32[]{:T(128)}, f32[256,256]{1,0:T(8,128)S(1)}, s32[2,2]{1,0:T(2,128)S(1)}, f32[2,128,128]{2,1,0:T(8,128)S(1)}, s32[]{:T(128)}) %tuple.103), condition=%wide.while_cond, body=%wide.while_body.sunk | while | flops 2 | bytes 131181 | solution.py:11
  319.4 0.6 fusion.68
  320.0 1.4 bitcast_dynamic-update-slice_fusion.6
  321.4 0.6 fusion.68
  322.0 1.4 bitcast_dynamic-update-slice_fusion.6
  323.4 19.7 %custom-call.16 = f32[2,128,128]{1,2,0:T(8,128)S(1)} custom-call(f32[2,128,128]{2,1,0:T(8,128)S(1)} %get-tuple-element.124), custom_call_target="InvertDiagBlocksLowerTriangular" | custom-call | tf_op jit(solution)/shard_map/jit(_cho_solve)/triangular_solve | solution.py:11
  343.1 0.9 fusion.23
  344.0 0.9 convolution_subtract_fusion.5
  344.9 0.3 fusion.25
  345.9 77.9 %psum.37 = f32[256]{0:T(256)S(1)} all-reduce(f32[256]{0:T(256)S(1)} %multiply_reduce_fusion.5), channel_id=1, replica_groups=mesh['ia'=4,'ja'=4,'ka'=16] {'ia','ja','ka'}, use_global_device_ids=true, to_apply=%region_13.16 | all-reduce | flops 256 | bytes 2048 | tf_op jit(solution)/shard_map/psum | solution.py:111
  423.9 0.6 bitcast_convert_fusion.4
  424.6 1.1 fusion.46
  425.8 71.7 %all-gather.6.cloned.1.call-done = bf16[2048,256]{1,0:T(8,128)(2,1)} async-done(((bf16[32,256]{1,0:T(8,128)(2,1)}), bf16[2048,256]{1,0:T(8,128)(2,1)}) %all-gather.6.cloned.1.call-update) | async-done | bytes 1048592 | tf_op jit(solution)/shard_map/all_gather | solution.py:116
  497.5 1.8 gather_fusion.2
  499.4 23.6 %conditional.6 = (f32[2048,256]{1,0:T(8,128)}) conditional(s32[]{:T(128)} %bitcast.41, () %tuple.57, (s32[1,1,1,2]{3,2,1,0:T(1,128)S(1)}, bf16[2048,256]{1,0:T(8,128)(2,1)S(1)}, bf16[1,1,1,2,128,128,128]{6,5,4,3,2,1,0:T(8,128)(2,1)}, s32[1,1,1,2]{3,2,1,0:T(1,128)S(1)}, bf16[512,256]{1,0:T(8,128)(2,1)S(1)}, ...), branch_computations={%region_15.18_spmd, %region_16.19_spmd} | conditional | flops 1082130432 | bytes 83099800 | solution.py:139
  499.4 2.5 slice.84
  501.9 3.6 convolution_bitcast_fusion.2
  505.5 6.7 copy.55
  512.4 8.3 multiply_reduce_fusion.2
  520.8 1.5 broadcast.142
  522.3 0.7 bitcast_dynamic-update-slice_fusion.3
  523.1 3.7 gather_fusion.3
  526.8 150.8 %all-reduce.5.cloned.1.call-done = f32[256,256]{0,1:T(8,128)} async-done(((f32[256,256]{0,1:T(8,128)}), f32[256,256]{0,1:T(8,128)}) %all-reduce.5.cloned.1.call-update) | async-done | bytes 262160 | tf_op jit(solution)/shard_map/psum | solution.py:115
  677.6 1.0 mul.96
  678.8 11.7 %cholesky.164 = f32[128,128]{1,0:T(8,128)S(1)} custom-call(f32[128,128]{1,0:T(8,128)S(1)} %cholesky.197), custom_call_target="Cholesky" | custom-call | tf_op jit(solution)/shard_map/jit(cholesky)/cholesky | solution.py:10
  690.6 9.8 %custom-call.17 = f32[1,128,128]{1,2,0:T(8,128)S(1)} custom-call(f32[1,128,128]{2,1,0:T(8,128)S(1)} %get-tuple-element.151), custom_call_target="InvertDiagBlocksLowerTriangular" | custom-call | tf_op jit(solution)/shard_map/jit(cholesky)/cholesky | solution.py:10
  700.9 11.7 %cholesky.181 = f32[128,128]{1,0:T(8,128)S(1)} custom-call(f32[128,128]{1,0:T(8,128)S(1)} %convolution_subtract_fusion), custom_call_target="Cholesky" | custom-call | tf_op jit(solution)/shard_map/jit(cholesky)/cholesky | solution.py:10
  712.6 0.6 compare_reduce_fusion
  713.3 0.6 compare_reduce_fusion.1
  715.2 4.2 while.5
  715.5 0.6 fusion.69
  716.1 1.4 bitcast_dynamic-update-slice_fusion.7
  717.5 0.6 fusion.69
  718.1 1.4 bitcast_dynamic-update-slice_fusion.7
  719.4 19.7 %custom-call.18 = f32[2,128,128]{1,2,0:T(8,128)S(1)} custom-call(f32[2,128,128]{2,1,0:T(8,128)S(1)} %get-tuple-element.125), custom_call_target="InvertDiagBlocksLowerTriangular" | custom-call | tf_op jit(solution)/shard_map/jit(_cho_solve)/triangular_solve | solution.py:11
  739.2 0.9 fusion.27
  740.0 0.9 convolution_subtract_fusion.3
  741.0 0.3 fusion.29
  742.0 77.3 %psum.39 = f32[256]{0:T(256)S(1)} all-reduce(f32[256]{0:T(256)S(1)} %multiply_reduce_fusion.4), channel_id=1, replica_groups=mesh['ia'=4,'ja'=4,'ka'=16] {'ia','ja','ka'}, use_global_device_ids=true, to_apply=%region_22.25 | all-reduce | flops 256 | bytes 2048 | tf_op jit(solution)/shard_map/psum | solution.py:145
  819.3 0.6 divide_bitcast_fusion
  (77 shorter events, 4.0 us)
Async XLA Ops:
  8.0 85.0 %all-gather.4.cloned.1.call-start = ((), (), s32[]{:S(2)}) async-start(), calls=%async_computation.2 | async-start | bytes 1064960 | tf_op jit(solution)/shard_map/all_gather | solution.py:80
  9.4 262.2 %all-reduce.7.cloned.1.call-start = ((), (), s32[]{:S(2)}) async-start(), calls=%async_computation.7 | async-start | bytes 1048576 | tf_op jit(solution)/shard_map/psum | solution.py:79
  13.5 329.6 %reduce-scatter.3.cloned.1.call-start = ((), (), s32[]{:S(2)}) async-start(), calls=%async_computation.3 | async-start | bytes 2129920 | tf_op jit(solution)/shard_map/reduce_scatter | solution.py:109
  100.7 6.7 copy-start.4
  107.5 8.4 %copy-start.7 = (s32[1,1,1,2]{3,2,1,0:T(1,128)S(1)}, s32[1,1,1,2]{3,2,1,0:T(1,128)}, u32[]{:S(2)}) copy-start(s32[1,1,1,2]{3,2,1,0:T(1,128)} %get-tuple-element.85) | copy-start | bytes 28 | tf_op jit(solution)/shard_map/cond
  121.7 302.8 %copy-start.1 = (s32[64]{0:T(128)S(1)}, s32[64]{0:T(128)}, u32[]{:S(2)}) copy-start(s32[64]{0:T(128)} %param.25) | copy-start | bytes 772
  121.8 375.7 %all-gather.6.cloned.1.call-start = ((), (), s32[]{:S(2)}) async-start(), calls=%async_computation.6 | async-start | bytes 1064960 | tf_op jit(solution)/shard_map/all_gather | solution.py:116
  271.6 227.7 %copy-start.2 = (s32[1,1,1,2]{3,2,1,0:T(1,128)S(1)}, s32[1,1,1,2]{3,2,1,0:T(1,128)}, u32[]{:S(2)}) copy-start(s32[1,1,1,2]{3,2,1,0:T(1,128)} %param.23) | copy-start | bytes 28
  271.6 227.7 %copy-start.3 = (s32[1,1,1,2]{3,2,1,0:T(1,128)S(1)}, s32[1,1,1,2]{3,2,1,0:T(1,128)}, u32[]{:S(2)}) copy-start(s32[1,1,1,2]{3,2,1,0:T(1,128)} %param.22) | copy-start | bytes 28
  271.6 227.7 %copy-start.6 = (s32[1,1,1,2]{3,2,1,0:T(1,128)S(1)}, s32[1,1,1,2]{3,2,1,0:T(1,128)}, u32[]{:S(2)}) copy-start(s32[1,1,1,2]{3,2,1,0:T(1,128)} %param.21) | copy-start | bytes 28
  424.5 253.1 %all-reduce.5.cloned.1.call-start = ((), (), s32[]{:S(2)}) async-start(), calls=%async_computation.4 | async-start | bytes 524288 | tf_op jit(solution)/shard_map/psum | solution.py:115
  425.8 313.4 %reduce-scatter.5.cloned.1.call-start = ((), (), s32[]{:S(2)}) async-start(), calls=%async_computation.5 | async-start | bytes 2129920 | tf_op jit(solution)/shard_map/reduce_scatter | solution.py:143
  523.1 154.5 %copy-start = (f32[256,256]{0,1:T(8,128)S(1)}, f32[256,256]{0,1:T(8,128)}, u32[]{:S(2)}) copy-start(f32[256,256]{0,1:T(8,128)} %get-tuple-element.143) | copy-start | bytes 786436
Sparse Core Ops, SparseCore 0:
  12.2 80.7 all-gather.3
  121.9 159.1 reduce-scatter.2
  424.6 72.8 all-gather.5
  527.0 159.5 reduce-scatter.4
Sparse Core Ops, SparseCore 1:
  15.6 256.0 all-reduce.6
  431.3 246.2 all-reduce.4
where the time goes:
time: 837 us; the launch traced here: 827 us
  waiting for transfers between devices  448 us (54%)
  blocking collectives  155 us (19%)
  other arithmetic  133 us (16%)
  local copies, waits for them, and re-layouts  42.5 us (5%)
  between operations  19.3 us (2%)
  matrix products  17.4 us (2%)
  loops' own time  12.2 us (1%)
    psum x1, waiting for transfers between devices, body(): gram_a = lax.psum(local_a, ('ia', 'ja', 'ka'))  151 us
    psum x1, waiting for transfers between devices, body(): gram_b, gram_c = lax.psum((local_b, local_c), ('ia', 'ja', 'ka'))  150 us
    psum x1, blocking collectives, body(): squares_a = lax.psum(jnp.sum(a_hat * a_hat, axis=0), ('ia', 'ja', 'ka'))  77.9 us
    psum x1, blocking collectives, body(): squares_b = lax.psum(jnp.sum(b_hat * b_hat, axis=0), ('ia', 'ja', 'ka'))  77.3 us
    all_gather x1, waiting for transfers between devices, body(): lax.all_gather(factor_b.astype(jnp.bfloat16), ('ia', 'ka'), axis=1, tiled...  75.5 us
    all_gather x1, waiting for transfers between devices, body(): lax.all_gather(a_own.astype(jnp.bfloat16)[None], ('ja', 'ka'), axis=1, ti...  71.7 us
    another operation x13, other arithmetic, solve_rows(): lower = jnp.linalg.cholesky(gram)  68.6 us
    another operation x5, other arithmetic, solve_rows(): return jax.scipy.linalg.cho_solve((lower, True), rows.T).T  39.4 us
  transfers between devices with their start and end apart: 6, of which 4 were waited for; matrix products, arithmetic and copies ran while one was open for 22% of the time, Pallas kernels for 0%

commit v1 on v0

--- a/solution.py
+++ b/solution.py
@@ -108,7 +108,7 @@
     system_one = gram_b * gram_c
     summed_own = lax.psum_scatter(stored_one, ("ja", "ka"), scatter_dimension=0, tiled=True)
     a_hat = solve_rows(system_one, summed_own)
-    squares_a = lax.psum(jnp.sum(a_hat * a_hat, axis=0), ("ia", "ja", "ka"))
+    squares_a = lax.psum(lax.psum(jnp.sum(a_hat * a_hat, axis=0), "ia"), ("ja", "ka"))
     scale_a = jnp.sqrt(squares_a / total_one + EPS)
     a_own = a_hat / scale_a
     local_a = jnp.dot(a_own.T, a_own, precision=highest, preferred_element_type=jnp.float32)

time: 837 us -> 881 us (1.053)
  blocking collectives: 155 us -> 214 us
  loops' own time: 12.2 us -> 1.74 us
    psum x1 -> x2, blocking collectives: 77.9 us -> 136 us  [the longest x1 128 us: body(): lax.psum(lax.psum(jnp.sum(a_hat * a_hat, axis=0), 'ia'), ('ja', 'ka'))]
    another operation x2, loops' own time: 10.9 us -> 0.53 us  [solve_rows(): return jax.scipy.linalg.cho_solve((lower, True), rows.T).T]
  transfers between devices with their start and end apart: 6 -> 6, of which waited for: 4 -> 4; matrix products, arithmetic and copies ran while one was open for 22% -> 21% of each run, Pallas kernels for 0% -> 0%
where the time goes in v1:
time: 881 us; the launch traced here: 872 us
  waiting for transfers between devices  444 us (50%)
  blocking collectives  214 us (24%)
  other arithmetic  133 us (15%)
  local copies, waits for them, and re-layouts  42.5 us (5%)
  between operations  19.3 us (2%)
  matrix products  17.4 us (2%)
    psum x1, waiting for transfers between devices, body(): gram_a = lax.psum(local_a, ('ia', 'ja', 'ka'))  150 us
    psum x1, waiting for transfers between devices, body(): gram_b, gram_c = lax.psum((local_b, local_c), ('ia', 'ja', 'ka'))  149 us
    psum x1, blocking collectives, body(): lax.psum(lax.psum(jnp.sum(a_hat * a_hat, axis=0), 'ia'), ('ja', 'ka'))  128 us
    psum x1, blocking collectives, body(): squares_b = lax.psum(jnp.sum(b_hat * b_hat, axis=0), ('ia', 'ja', 'ka'))  77.7 us
    all_gather x1, waiting for transfers between devices, body(): lax.all_gather(factor_b.astype(jnp.bfloat16), ('ia', 'ka'), axis=1, tiled...  75.5 us
    all_gather x1, waiting for transfers between devices, body(): lax.all_gather(a_own.astype(jnp.bfloat16)[None], ('ja', 'ka'), axis=1, ti...  68.8 us
    another operation x13, other arithmetic, solve_rows(): lower = jnp.linalg.cholesky(gram)  68.6 us
    another operation x5, other arithmetic, solve_rows(): return jax.scipy.linalg.cho_solve((lower, True), rows.T).T  39.4 us
  transfers between devices with their start and end apart: 6, of which 4 were waited for; matrix products, arithmetic and copies ran while one was open for 21% of the time, Pallas kernels for 0%

profile of v1, /device:TPU:1, one launch (start us, length us, event | category | flops | bytes accessed | tf_op | source)
XLA Modules:
  0.0 872.1 jit_solution(7007720908364222235)
XLA Ops:
  8.0 1.4 convert_element_type.36
  9.5 2.0 fusion.34
  11.5 2.0 fusion.36
  13.5 0.7 compare_select_fusion.3
  14.2 0.8 select_reduce_fusion.4
  14.9 0.8 select_reduce_fusion.5
  16.4 1.1 convert_bitcast_fusion
  17.5 75.5 %all-gather.4.cloned.1.call-done = bf16[1,2048,256]{2,1,0:T(8,128)(2,1)} async-done(((bf16[1,32,256]{2,1,0:T(8,128)(2,1)}), bf16[1,2048,256]{2,1,0:T(8,128)(2,1)}) %all-gather.4.cloned.1.call-update) | async-done | bytes 1048592 | tf_op jit(solution)/shard_map/all_gather | solution.py:80
  93.0 1.8 gather_fusion
  94.8 23.3 %conditional.4 = (f32[2048,256]{1,0:T(8,128)}) conditional(s32[]{:T(128)} %bitcast.41, () %tuple.54, (s32[1,1,1,2]{3,2,1,0:T(1,128)}, bf16[512,256]{1,0:T(8,128)(2,1)S(1)}, bf16[1,1,1,2,128,128,128]{6,5,4,3,2,1,0:T(8,128)(2,1)}, s32[1,1,1,2]{3,2,1,0:T(1,128)}, bf16[2048,256]{1,0:T(8,128)(2,1)S(1)}, /*index=5*/s32[1,1,1,2]{3,2,1,0:T(1,128)}) %tuple.134), branch_computations={%region_6.0_spmd, %region_7.0_spmd} | conditional | flops 1082130432 | bytes 83099928 | solution.py:104
  95.5 2.8 slice.76
  98.3 2.4 convolution_bitcast_fusion
  100.7 6.7 copy.52
  107.6 8.2 multiply_reduce_fusion
  116.0 1.5 broadcast.140
  117.4 0.7 bitcast_dynamic-update-slice_fusion.2
  118.1 3.6 gather_fusion.1
  121.8 0.6 all-gather.6.cloned.1.call-start
  122.3 149.3 %all-reduce.7.cloned.1.call-done = (f32[256,256]{0,1:T(8,128)}, f32[256,256]{0,1:T(8,128)}) async-done(((f32[256,256]{0,1:T(8,128)}, f32[256,256]{0,1:T(8,128)}), (f32[256,256]{0,1:T(8,128)}, f32[256,256]{0,1:T(8,128)})) %all-reduce.7.cloned.1.call-update) | async-done | bytes 524304 | tf_op jit(solution)/shard_map/psum | solution.py:79
  271.6 1.1 mul.94
  272.9 11.7 %cholesky.130 = f32[128,128]{1,0:T(8,128)S(1)} custom-call(f32[128,128]{1,0:T(8,128)S(1)} %cholesky.194), custom_call_target="Cholesky" | custom-call | tf_op jit(solution)/shard_map/jit(cholesky)/cholesky | solution.py:10
  284.7 9.8 %custom-call.15 = f32[1,128,128]{1,2,0:T(8,128)S(1)} custom-call(f32[1,128,128]{2,1,0:T(8,128)S(1)} %get-tuple-element.155), custom_call_target="InvertDiagBlocksLowerTriangular" | custom-call | tf_op jit(solution)/shard_map/jit(cholesky)/cholesky | solution.py:10
  295.0 11.7 %cholesky.147 = f32[128,128]{1,0:T(8,128)S(1)} custom-call(f32[128,128]{1,0:T(8,128)S(1)} %convolution_subtract_fusion.1), custom_call_target="Cholesky" | custom-call | tf_op jit(solution)/shard_map/jit(cholesky)/cholesky | solution.py:10
  306.7 0.7 compare_reduce_fusion.2
  308.8 4.1 while.4
  309.0 0.6 fusion.68
  309.6 1.4 bitcast_dynamic-update-slice_fusion.6
  311.0 0.6 fusion.68
  311.6 1.4 bitcast_dynamic-update-slice_fusion.6
  312.9 19.7 %custom-call.16 = f32[2,128,128]{1,2,0:T(8,128)S(1)} custom-call(f32[2,128,128]{2,1,0:T(8,128)S(1)} %get-tuple-element.124), custom_call_target="InvertDiagBlocksLowerTriangular" | custom-call | tf_op jit(solution)/shard_map/jit(_cho_solve)/triangular_solve | solution.py:11
  332.7 0.9 fusion.23
  333.5 0.9 convolution_subtract_fusion.5
  335.5 8.0 psum.44
  343.5 127.8 %psum.45 = f32[256]{0:T(256)S(1)} all-reduce(f32[256]{0:T(256)S(1)} %psum.44), channel_id=1, replica_groups=mesh['ia'=4,'ja'=4,'ka'=16] {'ja','ka'}, use_global_device_ids=true, to_apply=%region_14.17 | all-reduce | flops 256 | bytes 2048 | tf_op jit(solution)/shard_map/psum | solution.py:111
  471.3 0.6 bitcast_convert_fusion.4
  472.0 1.1 fusion.46
  473.3 68.8 %all-gather.6.cloned.1.call-done = bf16[2048,256]{1,0:T(8,128)(2,1)} async-done(((bf16[32,256]{1,0:T(8,128)(2,1)}), bf16[2048,256]{1,0:T(8,128)(2,1)}) %all-gather.6.cloned.1.call-update) | async-done | bytes 1048592 | tf_op jit(solution)/shard_map/all_gather | solution.py:116
  542.1 1.8 gather_fusion.2
  543.9 23.6 %conditional.6 = (f32[2048,256]{1,0:T(8,128)}) conditional(s32[]{:T(128)} %bitcast.41, () %tuple.57, (s32[1,1,1,2]{3,2,1,0:T(1,128)S(1)}, bf16[2048,256]{1,0:T(8,128)(2,1)S(1)}, bf16[1,1,1,2,128,128,128]{6,5,4,3,2,1,0:T(8,128)(2,1)}, s32[1,1,1,2]{3,2,1,0:T(1,128)S(1)}, bf16[512,256]{1,0:T(8,128)(2,1)S(1)}, ...), branch_computations={%region_16.19_spmd, %region_17.20_spmd} | conditional | flops 1082130432 | bytes 83099800 | solution.py:139
  544.0 2.5 slice.84
  546.5 3.6 convolution_bitcast_fusion.2
  550.1 6.7 copy.55
  557.0 8.3 multiply_reduce_fusion.2
  565.4 1.5 broadcast.142
  566.9 0.7 bitcast_dynamic-update-slice_fusion.3
  567.7 3.7 gather_fusion.3
  571.4 150.4 %all-reduce.5.cloned.1.call-done = f32[256,256]{0,1:T(8,128)} async-done(((f32[256,256]{0,1:T(8,128)}), f32[256,256]{0,1:T(8,128)}) %all-reduce.5.cloned.1.call-update) | async-done | bytes 262160 | tf_op jit(solution)/shard_map/psum | solution.py:115
  721.9 1.0 mul.96
  723.0 11.7 %cholesky.164 = f32[128,128]{1,0:T(8,128)S(1)} custom-call(f32[128,128]{1,0:T(8,128)S(1)} %cholesky.197), custom_call_target="Cholesky" | custom-call | tf_op jit(solution)/shard_map/jit(cholesky)/cholesky | solution.py:10
  734.8 9.8 %custom-call.17 = f32[1,128,128]{1,2,0:T(8,128)S(1)} custom-call(f32[1,128,128]{2,1,0:T(8,128)S(1)} %get-tuple-element.151), custom_call_target="InvertDiagBlocksLowerTriangular" | custom-call | tf_op jit(solution)/shard_map/jit(cholesky)/cholesky | solution.py:10
  745.1 11.7 %cholesky.181 = f32[128,128]{1,0:T(8,128)S(1)} custom-call(f32[128,128]{1,0:T(8,128)S(1)} %convolution_subtract_fusion), custom_call_target="Cholesky" | custom-call | tf_op jit(solution)/shard_map/jit(cholesky)/cholesky | solution.py:10
  756.9 0.6 compare_reduce_fusion
  757.5 0.6 compare_reduce_fusion.1
  759.5 4.2 while.5
  759.8 0.6 fusion.69
  760.3 1.4 bitcast_dynamic-update-slice_fusion.7
  761.7 0.6 fusion.69
  762.3 1.4 bitcast_dynamic-update-slice_fusion.7
  763.7 19.7 %custom-call.18 = f32[2,128,128]{1,2,0:T(8,128)S(1)} custom-call(f32[2,128,128]{2,1,0:T(8,128)S(1)} %get-tuple-element.125), custom_call_target="InvertDiagBlocksLowerTriangular" | custom-call | tf_op jit(solution)/shard_map/jit(_cho_solve)/triangular_solve | solution.py:11
  783.4 0.9 fusion.27
  784.3 0.9 convolution_subtract_fusion.3
  785.2 0.3 fusion.29
  786.2 77.7 %psum.47 = f32[256]{0:T(256)S(1)} all-reduce(f32[256]{0:T(256)S(1)} %multiply_reduce_fusion.4), channel_id=1, replica_groups=mesh['ia'=4,'ja'=4,'ka'=16] {'ia','ja','ka'}, use_global_device_ids=true, to_apply=%region_23.26 | all-reduce | flops 256 | bytes 2048 | tf_op jit(solution)/shard_map/psum | solution.py:145
  863.9 0.6 divide_bitcast_fusion
  (78 shorter events, 4.3 us)
Async XLA Ops:
  8.0 85.0 %all-gather.4.cloned.1.call-start = ((), (), s32[]{:S(2)}) async-start(), calls=%async_computation.2 | async-start | bytes 1064960 | tf_op jit(solution)/shard_map/all_gather | solution.py:80
  9.4 262.2 %all-reduce.7.cloned.1.call-start = ((), (), s32[]{:S(2)}) async-start(), calls=%async_computation.7 | async-start | bytes 1048576 | tf_op jit(solution)/shard_map/psum | solution.py:79
  13.5 319.2 %reduce-scatter.3.cloned.1.call-start = ((), (), s32[]{:S(2)}) async-start(), calls=%async_computation.3 | async-start | bytes 2129920 | tf_op jit(solution)/shard_map/reduce_scatter | solution.py:109
  100.7 6.7 copy-start.4
  107.5 8.4 copy-start.7
  121.7 350.3 %copy-start.1 = (s32[64]{0:T(128)S(1)}, s32[64]{0:T(128)}, u32[]{:S(2)}) copy-start(s32[64]{0:T(128)} %param.25) | copy-start | bytes 772
  121.8 420.3 %all-gather.6.cloned.1.call-start = ((), (), s32[]{:S(2)}) async-start(), calls=%async_computation.6 | async-start | bytes 1064960 | tf_op jit(solution)/shard_map/all_gather | solution.py:116
  271.6 272.3 %copy-start.2 = (s32[1,1,1,2]{3,2,1,0:T(1,128)S(1)}, s32[1,1,1,2]{3,2,1,0:T(1,128)}, u32[]{:S(2)}) copy-start(s32[1,1,1,2]{3,2,1,0:T(1,128)} %param.23) | copy-start | bytes 28
  271.6 272.3 %copy-start.3 = (s32[1,1,1,2]{3,2,1,0:T(1,128)S(1)}, s32[1,1,1,2]{3,2,1,0:T(1,128)}, u32[]{:S(2)}) copy-start(s32[1,1,1,2]{3,2,1,0:T(1,128)} %param.22) | copy-start | bytes 28
  271.6 272.3 %copy-start.6 = (s32[1,1,1,2]{3,2,1,0:T(1,128)S(1)}, s32[1,1,1,2]{3,2,1,0:T(1,128)}, u32[]{:S(2)}) copy-start(s32[1,1,1,2]{3,2,1,0:T(1,128)} %param.21) | copy-start | bytes 28
  471.9 249.9 %all-reduce.5.cloned.1.call-start = ((), (), s32[]{:S(2)}) async-start(), calls=%async_computation.4 | async-start | bytes 524288 | tf_op jit(solution)/shard_map/psum | solution.py:115
  473.2 310.2 %reduce-scatter.5.cloned.1.call-start = ((), (), s32[]{:S(2)}) async-start(), calls=%async_computation.5 | async-start | bytes 2129920 | tf_op jit(solution)/shard_map/reduce_scatter | solution.py:143
  567.7 154.1 %copy-start = (f32[256,256]{0,1:T(8,128)S(1)}, f32[256,256]{0,1:T(8,128)}, u32[]{:S(2)}) copy-start(f32[256,256]{0,1:T(8,128)} %get-tuple-element.143) | copy-start | bytes 786436
Sparse Core Ops, SparseCore 0:
  12.2 80.7 all-gather.3
  121.9 159.1 reduce-scatter.2
  472.1 69.9 all-gather.5
  571.5 159.6 reduce-scatter.4
Sparse Core Ops, SparseCore 1:
  15.6 256.0 all-reduce.6
  478.8 243.0 all-reduce.4
